TPU v7x, 512 devices: a whole 4x4x16 slice. The times are simulated.
512 devices in a mesh: row: 16 (over y, x), col: 32 (over z, core).
Axes of the slice: x: 4, y: 4, z: 16, core: 2. Of those that a mesh axis runs over, the one named last changes fastest.
Arguments:
- tokens: bfloat16 [4096, 8192], P('row', 'col'), may hold values from -6 to 6
- w_in: bfloat16 [8192, 3, 8192], P('row', None, 'col'), may hold values from -0.0625 to 0.0625
- filt_in: float32 [7, 3, 8192], P(None, None, 'col'), may hold values from -2.4 to 2.4
- filt_mix: float32 [7, 8192], P(None, 'col'), may hold values from -2.4 to 2.4
Outputs:
- gated: bfloat16 [4096, 8192], P('row', 'col')
All inputs are finite; a program needn't handle non-finite values.
Results may differ from a plain program's by a relative error of at most 0.0064.
Values may be sent and summed in bfloat16 or wider, within the bound.
A program may use at most 64 MiB of HBM per device.

v0:
```python
import jax
import jax.numpy as jnp
from jax import lax
from jax.sharding import PartitionSpec as P


def passed_along(block, axis, distance):
    devices = range(lax.axis_size(axis))
    route = [(i - distance, i) for i in devices if i - distance in devices]
    return lax.ppermute(block, axis, route)


def taps(ext, filt, count):
    total = filt[0] * ext[6 : 6 + count]
    for shift_s in range(1, 7):
        total = total + filt[shift_s] * ext[6 - shift_s : 6 - shift_s + count]
    return total


def per_device(tokens, w_in, filt_in, filt_mix):
    rows = tokens.shape[0]
    cols = w_in.shape[2]
    strip = lax.all_gather(tokens, "col", axis=1, tiled=True)
    piece = lax.all_gather(w_in, "row", axis=0, tiled=True)
    flat_piece = piece.reshape(piece.shape[0], 3 * cols)
    summed = jnp.dot(strip, flat_piece, preferred_element_type=jnp.float32)
    proj = summed.astype(jnp.bfloat16).reshape(rows, 3, cols)
    starts_seq = lax.axis_index("row") == 0
    keep_f = jnp.where(starts_seq, 0.0, 1.0).astype(jnp.float32)
    rim = passed_along(proj[rows - 6 :], "row", 1)
    ext = jnp.concatenate([rim.astype(jnp.float32) * keep_f, proj.astype(jnp.float32)], axis=0)
    conv = taps(ext, filt_in, rows)
    prod = conv[:, 1] * conv[:, 2]
    prod_rim = passed_along(prod[rows - 6 :], "row", 1)
    ext_prod = jnp.concatenate([prod_rim * keep_f, prod], axis=0)
    mix = taps(ext_prod, filt_mix, rows)
    query = conv[:, 0]
    return (query * mix).astype(jnp.bfloat16)


def solution(mesh):
    return jax.shard_map(
        per_device,
        mesh=mesh,
        in_specs=(P("row", "col"), P("row", None, "col"), P(None, None, "col"), P(None, "col")),
        out_specs=P("row", "col"),
        check_vma=False,
    )
```

profile of v0, /device:TPU:24, one launch (start us, length us, event | category | flops | bytes accessed | tf_op | source)
XLA Modules:
  0.0 247.5 jit_solution(13775816980189097958)
XLA Ops:
  6.5 0.0 all-gather.3.cloned.1.call-start
  6.5 0.7 all-gather.3.cloned.1.call-update
  7.3 0.0 all-gather.5.cloned.1.call-start
  7.3 2.3 copy.8
  9.6 0.0 all-gather.5.cloned.1.call-update
  9.6 1.0 fusion.36
  10.7 83.0 %all-gather.3.cloned.1.call-done = bf16[256,8192]{1,0:T(8,128)(2,1)} async-done(((bf16[256,256]{1,0:T(8,128)(2,1)}), bf16[256,8192]{1,0:T(8,128)(2,1)}) %all-gather.3.cloned.1.call-update) | async-done | bytes 4194320 | tf_op jit(solution)/shard_map/all_gather | solution.py:23
  93.7 114.1 %all-gather.5.cloned.1.call-done = bf16[8192,3,256]{0,2,1:T(8,128)(2,1)} async-done(((bf16[512,3,256]{0,2,1:T(8,128)(2,1)}), bf16[8192,3,256]{0,2,1:T(8,128)(2,1)}) %all-gather.5.cloned.1.call-update) | async-done | bytes 12582928 | tf_op jit(solution)/shard_map/all_gather | solution.py:24
  207.8 0.0 copy-start
  207.8 9.3 %convolution_convert_fusion = bf16[256,768]{1,0:T(8,128)(2,1)S(1)} fusion(bf16[256,8192]{1,0:T(8,128)(2,1)} %all-gather.3.cloned.1.call-done, bf16[8192,768]{0,1:T(8,128)(2,1)} %bitcast.45), kind=kOutput, calls=%fused_computation.10 | convolution fusion | flops 3221422080 | bytes 17170432 | tf_op jit(solution)/shard_map/dot_general | solution.py:26
  217.1 0.2 copy.12
  217.3 2.2 collective-permute-start
  219.5 0.0 copy-done
  219.5 0.2 copy.9
  219.7 7.4 %collective-permute-done = bf16[6,3,256]{0,2,1:T(8,128)(2,1)S(1)} collective-permute-done((bf16[6,3,256]{0,2,1:T(8,128)(2,1)S(1)}, bf16[6,3,256]{0,2,1:T(8,128)(2,1)S(1)}, u32[]{:S(2)}, u32[]{:S(2)}) %collective-permute-start) | collective-permute-done | bytes 9248 | tf_op jit(solution)/shard_map/ppermute | solution.py:10
  227.1 2.7 %fusion.3 = f32[256,3,256]{0,2,1:T(8,128)S(1)} fusion(f32[256,3,256]{0,2,1:T(8,128)S(1)} %bitcast.35, f32[6,3,256]{0,2,1:T(8,128)S(1)} %convert_multiply_fusion, f32[3,256]{1,0:T(4,128)S(1)} %get-tuple-element.19, f32[3,256]{1,0:T(4,128)S(1)} %get-tuple-element.20, f32[3,256]{1,0:T(4,128)S(1)} %get-tuple-element.21, f32[3,256]{1,0:T(4,128)S(1)} %get-tuple-element.22, ...), kind=kLoop, calls=%fused_computation.19 | loop fusion | flops 3735552 | bytes 1612800 | tf_op jit(solution)/shard_map/add | solution.py:16
  229.9 0.1 slice_bitcast_fusion.1
  230.0 1.9 collective-permute-start.1
  231.9 7.0 %collective-permute-done.1 = f32[6,256]{0,1:T(8,128)S(1)} collective-permute-done((f32[6,256]{0,1:T(8,128)S(1)}, f32[6,256]{0,1:T(8,128)S(1)}, u32[]{:S(2)}, u32[]{:S(2)}) %collective-permute-start.1) | collective-permute-done | bytes 6176 | tf_op jit(solution)/shard_map/ppermute | solution.py:10
  239.0 0.9 fusion.22
  239.9 0.8 copy.11
  (10 shorter events, 0.1 us)
Async XLA Ops:
  6.5 87.2 %all-gather.3.cloned.1.call-start = ((), (), s32[]{:S(2)}) async-start(), calls=%async_computation | async-start | bytes 4325376 | tf_op jit(solution)/shard_map/all_gather | solution.py:23
  7.3 200.6 %all-gather.5.cloned.1.call-start = ((), (), s32[]{:S(2)}) async-start(), calls=%async_computation.1 | async-start | bytes 13369344 | tf_op jit(solution)/shard_map/all_gather | solution.py:24
  207.8 11.7 %copy-start = (f32[7,256]{1,0:T(8,128)S(1)}, f32[7,256]{1,0:T(8,128)}, u32[]{:S(2)}) copy-start(f32[7,256]{1,0:T(8,128)} %param.7) | copy-start | bytes 21508
  217.3 9.8 %collective-permute-start = (bf16[6,3,256]{0,2,1:T(8,128)(2,1)S(1)}, bf16[6,3,256]{0,2,1:T(8,128)(2,1)S(1)}, u32[]{:S(2)}, u32[]{:S(2)}) collective-permute-start(bf16[6,3,256]{0,2,1:T(8,128)(2,1)S(1)} %bitcast.36), channel_id=1, source_target_pairs={{0,32},{32,64},{64,96},{96,128},{128,160},{160,192},{192,224},{224... | collective-permute-start | bytes 27656 | tf_op jit(solution)/shard_map/ppermute | solution.py:10
  230.0 9.0 %collective-permute-start.1 = (f32[6,256]{0,1:T(8,128)S(1)}, f32[6,256]{0,1:T(8,128)S(1)}, u32[]{:S(2)}, u32[]{:S(2)}) collective-permute-start(f32[6,256]{0,1:T(8,128)S(1)} %slice_bitcast_fusion.1), channel_id=1, source_target_pairs={{0,32},{32,64},{64,96},{96,128},{128,160},{160,192},{192,224},{224... | collective-permute-start | bytes 18440 | tf_op jit(solution)/shard_map/ppermute | solution.py:10
Sparse Core Ops, SparseCore 0:
  9.4 84.2 all-gather.2
  96.7 111.0 all-gather.4
where the time goes:
time: 248 us; the launch traced here: 247 us
  waiting for transfers between devices  212 us (85%)
  between operations  13.5 us (5%)
  matrix products  9.3 us (4%)
  local copies, waits for them, and re-layouts  4.56 us (2%)
  starting transfers between devices  4.13 us (2%)
  other arithmetic  3.72 us (2%)
    all_gather x1, waiting for transfers between devices, per_device(): piece = lax.all_gather(w_in, 'row', axis=0, tiled=True)  114 us
    all_gather x1, waiting for transfers between devices, per_device(): strip = lax.all_gather(tokens, 'col', axis=1, tiled=True)  83 us
    ppermute x2, waiting for transfers between devices, passed_along(): return lax.ppermute(block, axis, route)  14.4 us
    dot_general x1, matrix products, per_device(): summed = jnp.dot(strip, flat_piece, preferred_element_type=jnp.float32)  9.3 us
  transfers between devices with their start and end apart: 4, of which 4 were waited for; matrix products, arithmetic and copies ran while one was open for 1% of the time, Pallas kernels for 0%

commit v1 on v0

v1 whole, which is shorter than its diff:
```python
import jax
import jax.numpy as jnp
from jax import lax
from jax.experimental import pallas as pl
from jax.experimental.pallas import tpu as pltpu
from jax.sharding import PartitionSpec as P

MESH = pl.DeviceIdType.MESH
F32 = jnp.float32
BF16 = jnp.bfloat16

NX, NY, NZ = 4, 4, 16
TB = 256
EB = 256
WB = 512
CB = 256
HALO = 16
CHUNKS = (0, 1, 3, 2)
FAR_FIRST = (2, 1, 3)
WAVES = (
    (0, 0), (1, 0), (0, 1), (2, 0), (1, 1), (0, 2), (3, 0), (2, 1),
    (1, 2), (0, 3), (3, 1), (2, 2), (1, 3), (3, 2), (2, 3), (3, 3),
)
BEHIND = ((0, 4, -4, 8), (1, -3, 5, -7), (2, -2, 6, -6), (-1, 3, -5, 7))
GO_UP = ((1, 1, 0, 0), (1, 0, 1, 0), (1, 0, 1, 0), (0, 1, 0, 1))
GO_DOWN = ((1, 0, 1, 0), (0, 1, 0, 0), (0, 1, 0, 1), (1, 0, 1, 0))


def pick(table, m, slot):
    value = jnp.int32(table[3][slot])
    for case in (2, 1, 0):
        value = jnp.where(m == case, jnp.int32(table[case][slot]), value)
    return value


def kernel(
    tok_ref, w_ref, fin_ref, fmix_ref, out_ref,
    abuf, wbuf, part, landed, ext, prod,
    a_recv, a_sib, a_up, a_down, a_side, stage_sem,
    w_here, w_send, w_recv, p_send, p_recv, h_send, h_recv,
):
    row, col = lax.axis_index("row"), lax.axis_index("col")
    y, x = lax.div(row, 4), lax.rem(row, 4)
    z, core = lax.div(col, 2), lax.rem(col, 2)
    up = (row, lax.rem(z + 1, NZ) * 2 + core)
    down = (row, lax.rem(z + NZ - 1, NZ) * 2 + core)
    side = (row, z * 2 + 1 - core)
    y_next, y_prev = lax.rem(y + 1, NY), lax.rem(y + NY - 1, NY)
    north, south = (y_next * 4 + x, col), (y_prev * 4 + x, col)
    row_next, row_prev = (lax.rem(row + 1, 16), col), (lax.rem(row + 15, 16), col)
    across = [(y * 4 + lax.rem(x + d, NX), col) for d in (1, 2, 3)]

    barrier = pltpu.get_barrier_semaphore()
    greeted = [up, down, side, north, south, row_next, row_prev] + across
    for device in greeted:
        pl.semaphore_signal(barrier, inc=1, device_id=device, device_id_type=MESH)
    pl.semaphore_wait(barrier, len(greeted))

    def send(src, dst, send_sem, recv_sem, device):
        return pltpu.make_async_remote_copy(
            src_ref=src, dst_ref=dst, send_sem=send_sem, recv_sem=recv_sem,
            device_id=device, device_id_type=MESH,
        )

    m = lax.rem(z + NZ - x, 4)
    feeds = m == 0
    jz = lax.div(z, 4)
    home = abuf.at[jz, core, pl.ds(pl.multiple_of(x * TB, TB), TB)]
    stay = pltpu.make_async_copy(tok_ref, home, stage_sem.at[0])
    stage = send(tok_ref, home, stage_sem.at[1], a_recv.at[jz, x], (y * 4 + lax.rem(z, 4), col))

    @pl.when(feeds)
    def _():
        stay.start()

    @pl.when(jnp.logical_not(feeds))
    def _():
        stage.start()

    def w_rows(block, half):
        return wbuf.at[pl.ds(pl.multiple_of(block * WB + half * (WB // 2), WB // 2), WB // 2)]

    def own_half(half):
        return w_ref.at[pl.ds(half * (WB // 2), WB // 2)]

    w_stay = pltpu.make_async_copy(w_ref, wbuf.at[pl.ds(pl.multiple_of(y * WB, WB), WB)], w_here)
    w_sends = []
    for turn in range(2):
        for way, device in ((0, north), (1, south)):
            half = turn if way == 0 else 1 - turn
            w_sends.append(send(own_half(half), w_rows(y, half), w_send.at[way, half], w_recv.at[way, half], device))
    for copy in w_sends:
        copy.start()
    w_stay.start()
    on_north = send(w_rows(y_prev, 0), w_rows(y_prev, 0), w_send.at[2, 0], w_recv.at[2, 0], north)
    on_south = send(w_rows(y_next, 1), w_rows(y_next, 1), w_send.at[2, 1], w_recv.at[2, 1], south)

    def w_arrival(way, half, block):
        return send(w_rows(block, half), w_rows(block, half), w_send.at[way, half], w_recv.at[way, half], north)

    @pl.when(feeds)
    def _():
        stay.wait()

    drains = []
    for place, (chunk, slot) in enumerate(WAVES):
        if place == 6:
            w_arrival(0, 0, y_prev).wait_recv()
            on_north.start()
            w_arrival(1, 1, y_next).wait_recv()
            on_south.start()
        k = lax.rem(x + CHUNKS[chunk], 4)
        j = lax.div(lax.rem(z + 2 * NZ - x - pick(BEHIND, m, slot), NZ), 4)
        piece = abuf.at[j, core, pl.ds(pl.multiple_of(k * TB, TB), TB)]
        go_up, go_down = pick(GO_UP, m, slot) == 1, pick(GO_DOWN, m, slot) == 1
        on_up = send(piece, piece, a_up.at[chunk, slot], a_recv.at[j, k], up)
        on_down = send(piece, piece, a_down.at[chunk, slot], a_recv.at[j, k], down)
        on_side = send(piece, piece, a_side.at[chunk, slot], a_sib.at[j, k], side)
        if chunk == 0 and slot == 0:
            @pl.when(jnp.logical_not(feeds))
            def _():
                on_up.wait_recv()
        else:
            on_up.wait_recv()

        @pl.when(go_up)
        def _():
            on_up.start()

        @pl.when(go_down)
        def _():
            on_down.start()

        on_side.start()
        drains.append((go_up, on_up, go_down, on_down, on_side))

    w_stay.wait()
    w_arrival(0, 1, y_prev).wait_recv()
    w_arrival(1, 0, y_next).wait_recv()
    far = lax.rem(y + 2, NY)
    w_arrival(2, 0, far).wait_recv()
    w_arrival(2, 1, far).wait_recv()
    for j in range(4):
        for k in range(4):
            piece = abuf.at[j, 1 - core, pl.ds(k * TB, TB)]
            send(piece, piece, a_side.at[j, k], a_sib.at[j, k], side).wait_recv()

    def partial(k):
        rows = pl.ds(pl.multiple_of(k * TB, TB), TB)
        strip = jnp.concatenate([abuf[j, h, rows, :] for j in range(4) for h in range(2)], axis=1)
        return jnp.dot(strip, wbuf[...], preferred_element_type=F32)

    shares = []
    for i, distance in enumerate(FAR_FIRST):
        part[i] = partial(lax.rem(x + distance, NX)).astype(BF16)
        share = send(part.at[i], landed.at[i], p_send.at[i], p_recv.at[i], across[distance - 1])
        share.start()
        shares.append(share)
    ext[HALO:, :] = partial(x)
    for i in (1, 2, 0):
        shares[i].wait_recv()
    ext[HALO:, :] = ext[HALO:, :] + ((landed[1].astype(F32) + landed[2].astype(F32)) + landed[0].astype(F32))

    halo = send(ext.at[pl.ds(TB, HALO)], ext.at[pl.ds(0, HALO)], h_send, h_recv, row_next)
    halo.start()
    halo.wait()

    @pl.when(row == 0)
    def _():
        ext[:HALO, :] = jnp.zeros((HALO, 3 * CB), F32)

    def taps(group, lanes, first, count):
        at = pl.ds(group * CB + lanes, 128)
        total = fin_ref[0:1, at] * ext[first : first + count, at]
        for s in range(1, 7):
            total = total + fin_ref[s : s + 1, at] * ext[first - s : first - s + count, at]
        return total

    for lanes in range(0, CB, 128):
        at = pl.ds(lanes, 128)
        prod[:, at] = taps(1, lanes, 8, TB + 8) * taps(2, lanes, 8, TB + 8)
        mix = fmix_ref[0:1, at] * prod[8 : 8 + TB, at]
        for s in range(1, 7):
            mix = mix + fmix_ref[s : s + 1, at] * prod[8 - s : 8 - s + TB, at]
        out_ref[:, at] = (taps(0, lanes, HALO, TB) * mix).astype(BF16)

    for share in shares:
        share.wait_send()
    for copy in w_sends + [on_north, on_south]:
        copy.wait_send()

    @pl.when(jnp.logical_not(feeds))
    def _():
        stage.wait_send()

    for go_up, on_up, go_down, on_down, on_side in drains:
        pl.when(go_up)(on_up.wait_send)
        pl.when(go_down)(on_down.wait_send)
        on_side.wait_send()


def per_device(tokens, w_in, filt_in, filt_mix):
    vmem = pl.BlockSpec(memory_space=pltpu.VMEM)
    dma = pltpu.SemaphoreType.DMA
    return pl.pallas_call(
        kernel,
        out_shape=jax.ShapeDtypeStruct((TB, CB), BF16),
        in_specs=[vmem] * 4,
        out_specs=vmem,
        scratch_shapes=[
            pltpu.VMEM((4, 2, NX * TB, EB), BF16),
            pltpu.VMEM((NY * WB, 3 * CB), BF16),
            pltpu.VMEM((3, TB, 3 * CB), BF16),
            pltpu.VMEM((3, TB, 3 * CB), BF16),
            pltpu.VMEM((HALO + TB, 3 * CB), F32),
            pltpu.VMEM((TB + 8, CB), F32),
            dma((4, 4)), dma((4, 4)), dma((4, 4)), dma((4, 4)), dma((4, 4)), dma((2,)),
            dma, dma((3, 2)), dma((3, 2)), dma((3,)), dma((3,)), dma, dma,
        ],
        compiler_params=pltpu.CompilerParams(collective_id=0, has_side_effects=True),
    )(tokens, w_in.reshape(WB, 3 * CB), filt_in.reshape(7, 3 * CB), filt_mix)


def solution(mesh):
    return jax.shard_map(
        per_device,
        mesh=mesh,
        in_specs=(P("row", "col"), P("row", None, "col"), P(None, None, "col"), P(None, "col")),
        out_specs=P("row", "col"),
        check_vma=False,
    )
```

time: 248 us -> 122 us (0.49)
  the two profiles are of different devices: /device:TPU:24 before, /device:TPU:1 now
where the time goes in v1:
time: 122 us; the launch traced here: 120 us
  Pallas kernels  116 us (95%)
  local copies, waits for them, and re-layouts  4.13 us (3%)
    pallas_call x1, Pallas kernels, per_device(): pl.pallas_call(kernel, out_shape=jax.ShapeDtypeStruct((TB, CB), BF16), in...  116 us
    unnamed x2, local copies, waits for them, and re-layouts  2.98 us

profile of v1, /device:TPU:1, one launch (start us, length us, event | category | flops | bytes accessed | tf_op | source)
XLA Modules:
  0.0 120.5 jit_solution(16317988581132363605)
XLA Ops:
  0.0 1.4 %copy.6 = bf16[512,3,256]{0,2,1:T(8,128)(2,1)S(1)} copy(bf16[512,3,256]{2,0,1:T(8,128)(2,1)} %param.5) | data formatting | bytes 1572864 | tf_op args[1]
  1.4 1.2 copy.7.w_ref
  2.6 116.3 %shard_map.46 = bf16[256,256]{1,0:T(8,128)(2,1)} custom-call(bf16[256,256]{1,0:T(8,128)(2,1)} %tok_ref.1, bf16[512,768]{1,0:T(8,128)(2,1)} %copy.7.w_ref, f32[7,768]{1,0:T(8,128)} %bitcast.3, f32[7,256]{1,0:T(8,128)} %fmix_ref.1), custom_call_target="tpu_custom_call" | custom-call | tf_op jit(solution)/shard_map/pallas_call | solution.py:205
  118.9 1.6 %copy.9 = bf16[256,256]{1,0:T(8,128)(2,1)} copy(bf16[256,256]{1,0:T(8,128)(2,1)} %shard_map.46) | data formatting | bytes 262144

commit v2 on v1

v2 whole, which is shorter than its diff:
```python
import jax
import jax.numpy as jnp
from jax import lax
from jax.experimental import pallas as pl
from jax.experimental.pallas import tpu as pltpu
from jax.sharding import PartitionSpec as P

MESH = pl.DeviceIdType.MESH
F32 = jnp.float32
BF16 = jnp.bfloat16

NX, NY, NZ = 4, 4, 16
TB = 256
EB = 256
WB = 512
CB = 256
HALO = 16
FAR_FIRST = (2, 1, 3)
W_HOP = 2
CUTS = 2
PT = TB // CUTS
UP, DOWN = NZ // 2, NZ // 2 - 1


def kernel(
    tok_ref, w_ref, fin_ref, fmix_ref, out_ref,
    abuf, wbuf, part, landed, ext, prod,
    stage_sem, stage_send, stage_recv, a_send, a_recv, s_send, s_recv,
    w_here, w_send, w_recv, p_send, p_recv, h_send, h_recv,
):
    row, col = lax.axis_index("row"), lax.axis_index("col")
    y, x = lax.div(row, 4), lax.rem(row, 4)
    z, core = lax.div(col, 2), lax.rem(col, 2)
    up = (row, lax.rem(z + 1, NZ) * 2 + core)
    down = (row, lax.rem(z + NZ - 1, NZ) * 2 + core)
    side = (row, z * 2 + 1 - core)
    y_next, y_prev = lax.rem(y + 1, NY), lax.rem(y + NY - 1, NY)
    north, south = (y_next * 4 + x, col), (y_prev * 4 + x, col)
    row_next, row_prev = (lax.rem(row + 1, 16), col), (lax.rem(row + 15, 16), col)
    across = [(y * 4 + lax.rem(x + d, NX), col) for d in (1, 2, 3)]

    twin_x, twin_z = lax.rem(z, 4), lax.div(z, 4) * 4 + x
    twin = (y * 4 + twin_x, twin_z * 2 + core)
    alone = twin_x == x

    barrier = pltpu.get_barrier_semaphore()
    greeted = [up, down, side, north, south, row_next, row_prev] + across
    for device in greeted:
        pl.semaphore_signal(barrier, inc=1, device_id=device, device_id_type=MESH)

    @pl.when(jnp.logical_not(alone))
    def _():
        pl.semaphore_signal(barrier, inc=1, device_id=twin, device_id_type=MESH)

    pl.semaphore_wait(barrier, len(greeted) + 1 - alone.astype(jnp.int32))

    def send(src, dst, send_sem, recv_sem, device):
        return pltpu.make_async_remote_copy(
            src_ref=src, dst_ref=dst, send_sem=send_sem, recv_sem=recv_sem,
            device_id=device, device_id_type=MESH,
        )

    def piece(block, half, cut):
        return abuf.at[block, half, pl.ds(cut * PT, PT)]

    stay = pltpu.make_async_copy(tok_ref, abuf.at[z, core], stage_sem)
    swaps = [
        send(
            tok_ref.at[pl.ds(cut * PT, PT)], piece(twin_z, core, cut),
            stage_send.at[cut], stage_recv.at[cut], twin,
        )
        for cut in range(CUTS)
    ]

    @pl.when(alone)
    def _():
        stay.start()

    @pl.when(jnp.logical_not(alone))
    def _():
        for copy in swaps:
            copy.start()

    def w_rows(block, half):
        return wbuf.at[:, pl.ds(pl.multiple_of(block * WB + half * (WB // 2), WB // 2), WB // 2)]

    def own_half(half):
        return w_ref.at[:, pl.ds(half * (WB // 2), WB // 2)]

    w_stay = pltpu.make_async_copy(w_ref, wbuf.at[:, pl.ds(pl.multiple_of(y * WB, WB), WB)], w_here)
    w_sends = []
    for turn in range(2):
        for way, device in ((0, north), (1, south)):
            half = turn if way == 0 else 1 - turn
            w_sends.append(send(own_half(half), w_rows(y, half), w_send.at[way, half], w_recv.at[way, half], device))
    for copy in w_sends:
        copy.start()
    w_stay.start()
    on_north = send(w_rows(y_prev, 0), w_rows(y_prev, 0), w_send.at[2, 0], w_recv.at[2, 0], north)
    on_south = send(w_rows(y_next, 1), w_rows(y_next, 1), w_send.at[2, 1], w_recv.at[2, 1], south)

    def w_arrival(way, half, block):
        return send(w_rows(block, half), w_rows(block, half), w_send.at[way, half], w_recv.at[way, half], north)

    @pl.when(alone)
    def _():
        stay.wait()

    sent = []

    def pass_on(way, hop, cut):
        block = lax.rem(z + NZ - hop if way == 0 else z + hop, NZ)
        here = piece(block, core, cut)
        limit, device = (UP, up) if way == 0 else (DOWN, down)
        if hop:
            send(here, here, a_send.at[way, 0, cut], a_recv.at[way, hop - 1, cut], device).wait_recv()
        if hop < limit:
            on = send(here, here, a_send.at[way, hop, cut], a_recv.at[way, hop, cut], device)
            on.start()
            sent.append(on)
        if hop or way == 0:
            place = hop if way == 0 else UP + hop
            to_side = send(here, here, s_send.at[place, cut], s_recv.at[block, cut], side)
            to_side.start()
            sent.append(to_side)

    for hop in range(UP + 1):
        for cut in range(CUTS):
            if hop == 0:
                @pl.when(jnp.logical_not(alone))
                def _():
                    send(piece(z, core, cut), piece(z, core, cut), stage_send.at[cut], stage_recv.at[cut], twin).wait_recv()
            pass_on(0, hop, cut)
            if hop <= DOWN:
                pass_on(1, hop, cut)
        if hop == W_HOP:
            w_arrival(0, 0, y_prev).wait_recv()
            on_north.start()
            w_arrival(1, 1, y_next).wait_recv()
            on_south.start()

    w_stay.wait()
    w_arrival(0, 1, y_prev).wait_recv()
    w_arrival(1, 0, y_next).wait_recv()
    far = lax.rem(y + 2, NY)
    w_arrival(2, 0, far).wait_recv()
    w_arrival(2, 1, far).wait_recv()
    for block in range(NZ):
        for cut in range(CUTS):
            there = piece(block, 1 - core, cut)
            send(there, there, s_send.at[block, cut], s_recv.at[block, cut], side).wait_recv()

    def partial(k):
        strip = jnp.concatenate([abuf[j * 4 + k, h] for j in range(4) for h in range(2)], axis=1)
        return [jnp.dot(strip, wbuf[g], preferred_element_type=F32) for g in range(3)]

    shares = []
    for i, distance in enumerate(FAR_FIRST):
        for g, product in enumerate(partial(lax.rem(x + distance, NX))):
            part[i, :, g * CB : (g + 1) * CB] = product.astype(BF16)
        share = send(part.at[i], landed.at[i], p_send.at[i], p_recv.at[i], across[distance - 1])
        share.start()
        shares.append(share)
    for g, product in enumerate(partial(x)):
        ext[HALO:, g * CB : (g + 1) * CB] = product
    for i in (1, 2, 0):
        shares[i].wait_recv()
    ext[HALO:, :] = ext[HALO:, :] + ((landed[1].astype(F32) + landed[2].astype(F32)) + landed[0].astype(F32))

    halo = send(ext.at[pl.ds(TB, HALO)], ext.at[pl.ds(0, HALO)], h_send, h_recv, row_next)
    halo.start()
    halo.wait()

    @pl.when(row == 0)
    def _():
        ext[:HALO, :] = jnp.zeros((HALO, 3 * CB), F32)

    def taps(group, lanes, first, count):
        at = pl.ds(group * CB + lanes, 128)
        own = pl.ds(lanes, 128)
        total = fin_ref[group, 0:1, own] * ext[first : first + count, at]
        for s in range(1, 7):
            total = total + fin_ref[group, s : s + 1, own] * ext[first - s : first - s + count, at]
        return total

    for lanes in range(0, CB, 128):
        at = pl.ds(lanes, 128)
        prod[:, at] = taps(1, lanes, 8, TB + 8) * taps(2, lanes, 8, TB + 8)
        mix = fmix_ref[0:1, at] * prod[8 : 8 + TB, at]
        for s in range(1, 7):
            mix = mix + fmix_ref[s : s + 1, at] * prod[8 - s : 8 - s + TB, at]
        out_ref[:, at] = (taps(0, lanes, HALO, TB) * mix).astype(BF16)

    for share in shares:
        share.wait_send()
    for copy in w_sends + [on_north, on_south]:
        copy.wait_send()

    @pl.when(jnp.logical_not(alone))
    def _():
        for copy in swaps:
            copy.wait_send()

    for copy in sent:
        copy.wait_send()


def per_device(tokens, w_in, filt_in, filt_mix):
    vmem = pl.BlockSpec(memory_space=pltpu.VMEM)
    dma = pltpu.SemaphoreType.DMA
    return pl.pallas_call(
        kernel,
        out_shape=jax.ShapeDtypeStruct((TB, CB), BF16),
        in_specs=[vmem] * 4,
        out_specs=vmem,
        scratch_shapes=[
            pltpu.VMEM((NZ, 2, TB, EB), BF16),
            pltpu.VMEM((3, NY * WB, CB), BF16),
            pltpu.VMEM((3, TB, 3 * CB), BF16),
            pltpu.VMEM((3, TB, 3 * CB), BF16),
            pltpu.VMEM((HALO + TB, 3 * CB), F32),
            pltpu.VMEM((TB + 8, CB), F32),
            dma, dma((CUTS,)), dma((CUTS,)), dma((2, UP, CUTS)), dma((2, UP, CUTS)), dma((NZ, CUTS)), dma((NZ, CUTS)),
            dma, dma((3, 2)), dma((3, 2)), dma((3,)), dma((3,)), dma, dma,
        ],
        compiler_params=pltpu.CompilerParams(collective_id=0, has_side_effects=True),
    )(tokens, jnp.transpose(w_in, (1, 0, 2)), jnp.transpose(filt_in, (1, 0, 2)), filt_mix)


def solution(mesh):
    return jax.shard_map(
        per_device,
        mesh=mesh,
        in_specs=(P("row", "col"), P("row", None, "col"), P(None, None, "col"), P(None, "col")),
        out_specs=P("row", "col"),
        check_vma=False,
    )
```

time: 122 us -> 86.5 us (0.71); the launches traced: 120 us -> 86.4 us
  Pallas kernels: 116 us -> 84.8 us
  local copies, waits for them, and re-layouts: 4.13 us -> 1.57 us
    pallas_call x1, Pallas kernels: 116 us -> 84.8 us  [per_device(): pl.pallas_call(kernel, out_shape=jax.ShapeDtypeStruct((TB, CB), BF16), in...]
    unnamed x2 -> x1, local copies, waits for them, and re-layouts: 2.98 us -> 1.57 us
where the time goes in v2:
time: 86.5 us; the launch traced here: 86.4 us
  Pallas kernels  84.8 us (98%)
  local copies, waits for them, and re-layouts  1.57 us (2%)
    pallas_call x1, Pallas kernels, per_device(): pl.pallas_call(kernel, out_shape=jax.ShapeDtypeStruct((TB, CB), BF16), in...  84.8 us

profile of v2, /device:TPU:1, one launch (start us, length us, event | category | flops | bytes accessed | tf_op | source)
XLA Modules:
  0.0 86.4 jit_solution(11477180028568045373)
XLA Ops:
  0.0 84.8 %shard_map.46 = bf16[256,256]{1,0:T(8,128)(2,1)} custom-call(bf16[256,256]{1,0:T(8,128)(2,1)} %tok_ref.1, bf16[3,512,256]{2,1,0:T(8,128)(2,1)} %bitcast.2, f32[3,7,256]{2,1,0:T(8,128)} %bitcast.3, f32[7,256]{1,0:T(8,128)} %fmix_ref.1), custom_call_target="tpu_custom_call" | custom-call | tf_op jit(solution)/shard_map/pallas_call | solution.py:211
  84.8 1.6 %copy.6 = bf16[256,256]{1,0:T(8,128)(2,1)} copy(bf16[256,256]{1,0:T(8,128)(2,1)} %shard_map.46) | data formatting | bytes 262144

commit v3 on v2

--- a/solution.py
+++ b/solution.py
@@ -16,17 +16,17 @@
 CB = 256
 HALO = 16
 FAR_FIRST = (2, 1, 3)
-W_HOP = 2
-CUTS = 2
+W_HOP = 1
+CUTS = 4
 PT = TB // CUTS
 UP, DOWN = NZ // 2, NZ // 2 - 1
 
 
 def kernel(
     tok_ref, w_ref, fin_ref, fmix_ref, out_ref,
-    abuf, wbuf, part, landed, ext, prod,
+    abuf, wbuf, part, landed, rim_part, rim_land, ext, prod,
     stage_sem, stage_send, stage_recv, a_send, a_recv, s_send, s_recv,
-    w_here, w_send, w_recv, p_send, p_recv, h_send, h_recv,
+    w_here, w_send, w_recv, p_send, p_recv, r_send, r_recv,
 ):
     row, col = lax.axis_index("row"), lax.axis_index("col")
     y, x = lax.div(row, 4), lax.rem(row, 4)
@@ -36,7 +36,8 @@
     side = (row, z * 2 + 1 - core)
     y_next, y_prev = lax.rem(y + 1, NY), lax.rem(y + NY - 1, NY)
     north, south = (y_next * 4 + x, col), (y_prev * 4 + x, col)
-    row_next, row_prev = (lax.rem(row + 1, 16), col), (lax.rem(row + 15, 16), col)
+    heir = (y_next * 4, col)
+    first = x == 0
     across = [(y * 4 + lax.rem(x + d, NX), col) for d in (1, 2, 3)]
 
     twin_x, twin_z = lax.rem(z, 4), lax.div(z, 4) * 4 + x
@@ -44,15 +45,20 @@
     alone = twin_x == x
 
     barrier = pltpu.get_barrier_semaphore()
-    greeted = [up, down, side, north, south, row_next, row_prev] + across
-    for device in greeted:
+    greeted = [up, down, side, north, south] + across
+    for device in greeted + [heir]:
         pl.semaphore_signal(barrier, inc=1, device_id=device, device_id_type=MESH)
 
     @pl.when(jnp.logical_not(alone))
     def _():
         pl.semaphore_signal(barrier, inc=1, device_id=twin, device_id_type=MESH)
 
-    pl.semaphore_wait(barrier, len(greeted) + 1 - alone.astype(jnp.int32))
+    @pl.when(first)
+    def _():
+        for x_from in range(NX):
+            pl.semaphore_signal(barrier, inc=1, device_id=(y_prev * 4 + x_from, col), device_id_type=MESH)
+
+    pl.semaphore_wait(barrier, len(greeted) + 2 - alone.astype(jnp.int32) + 4 * first.astype(jnp.int32))
 
     def send(src, dst, send_sem, recv_sem, device):
         return pltpu.make_async_remote_copy(
@@ -150,26 +156,55 @@
             there = piece(block, 1 - core, cut)
             send(there, there, s_send.at[block, cut], s_recv.at[block, cut], side).wait_recv()
 
+    def product(strip):
+        return [jnp.dot(strip, wbuf[g], preferred_element_type=F32) for g in range(3)]
+
     def partial(k):
         strip = jnp.concatenate([abuf[j * 4 + k, h] for j in range(4) for h in range(2)], axis=1)
-        return [jnp.dot(strip, wbuf[g], preferred_element_type=F32) for g in range(3)]
+        return product(strip)
+
+    tails = jnp.concatenate(
+        [
+            jnp.concatenate([abuf[j * 4 + k, h, TB - HALO :, :] for k in range(NX)], axis=0)
+            for j in range(4)
+            for h in range(2)
+        ],
+        axis=1,
+    )
+    for g, rows in enumerate(product(tails)):
+        for k in range(NX):
+            rim_part[k, :, g * CB : (g + 1) * CB] = rows[k * HALO : (k + 1) * HALO].astype(BF16)
+    rims = []
+    for d in (2, 1, 3):
+        x_to = lax.rem(x + d, NX)
+        y_to = lax.rem(y + (x_to == 0).astype(jnp.int32), NY)
+        rims.append(send(rim_part.at[lax.rem(x_to + 3, NX)], rim_land.at[d], r_send.at[d], r_recv.at[d], (y_to * 4 + x_to, col)))
+    own_rim = send(rim_part.at[3], rim_land.at[0], r_send.at[0], r_recv.at[0], heir)
+    for rim in rims:
+        rim.start()
+    pl.when(first)(own_rim.start)
 
     shares = []
     for i, distance in enumerate(FAR_FIRST):
-        for g, product in enumerate(partial(lax.rem(x + distance, NX))):
-            part[i, :, g * CB : (g + 1) * CB] = product.astype(BF16)
+        for g, block in enumerate(partial(lax.rem(x + distance, NX))):
+            part[i, :, g * CB : (g + 1) * CB] = block.astype(BF16)
         share = send(part.at[i], landed.at[i], p_send.at[i], p_recv.at[i], across[distance - 1])
         share.start()
         shares.append(share)
-    for g, product in enumerate(partial(x)):
-        ext[HALO:, g * CB : (g + 1) * CB] = product
+    for g, block in enumerate(partial(x)):
+        ext[HALO:, g * CB : (g + 1) * CB] = block
     for i in (1, 2, 0):
         shares[i].wait_recv()
     ext[HALO:, :] = ext[HALO:, :] + ((landed[1].astype(F32) + landed[2].astype(F32)) + landed[0].astype(F32))
 
-    halo = send(ext.at[pl.ds(TB, HALO)], ext.at[pl.ds(0, HALO)], h_send, h_recv, row_next)
-    halo.start()
-    halo.wait()
+    @pl.when(jnp.logical_not(first))
+    def _():
+        rim_land[0] = rim_part[lax.rem(x + 3, NX)]
+
+    pl.when(first)(own_rim.wait_recv)
+    for rim in rims:
+        rim.wait_recv()
+    ext[:HALO, :] = (rim_land[0].astype(F32) + rim_land[1].astype(F32)) + (rim_land[2].astype(F32) + rim_land[3].astype(F32))
 
     @pl.when(row == 0)
     def _():
@@ -191,8 +226,9 @@
             mix = mix + fmix_ref[s : s + 1, at] * prod[8 - s : 8 - s + TB, at]
         out_ref[:, at] = (taps(0, lanes, HALO, TB) * mix).astype(BF16)
 
-    for share in shares:
+    for share in shares + rims:
         share.wait_send()
+    pl.when(first)(own_rim.wait_send)
     for copy in w_sends + [on_north, on_south]:
         copy.wait_send()
 
@@ -218,10 +254,12 @@
             pltpu.VMEM((3, NY * WB, CB), BF16),
             pltpu.VMEM((3, TB, 3 * CB), BF16),
             pltpu.VMEM((3, TB, 3 * CB), BF16),
+            pltpu.VMEM((NX, HALO, 3 * CB), BF16),
+            pltpu.VMEM((NX, HALO, 3 * CB), BF16),
             pltpu.VMEM((HALO + TB, 3 * CB), F32),
             pltpu.VMEM((TB + 8, CB), F32),
             dma, dma((CUTS,)), dma((CUTS,)), dma((2, UP, CUTS)), dma((2, UP, CUTS)), dma((NZ, CUTS)), dma((NZ, CUTS)),
-            dma, dma((3, 2)), dma((3, 2)), dma((3,)), dma((3,)), dma, dma,
+            dma, dma((3, 2)), dma((3, 2)), dma((3,)), dma((3,)), dma((NX,)), dma((NX,)),
         ],
         compiler_params=pltpu.CompilerParams(collective_id=0, has_side_effects=True),
     )(tokens, jnp.transpose(w_in, (1, 0, 2)), jnp.transpose(filt_in, (1, 0, 2)), filt_mix)

time: 86.5 us -> 81.4 us (0.941)
  Pallas kernels: 84.8 us -> 79.6 us
    pallas_call x1, Pallas kernels: 84.8 us -> 79.6 us  [per_device(): pl.pallas_call(kernel, out_shape=jax.ShapeDtypeStruct((TB, CB), BF16), in...]
where the time goes in v3:
time: 81.4 us; the launch traced here: 81.2 us
  Pallas kernels  79.6 us (98%)
  local copies, waits for them, and re-layouts  1.57 us (2%)
    pallas_call x1, Pallas kernels, per_device(): pl.pallas_call(kernel, out_shape=jax.ShapeDtypeStruct((TB, CB), BF16), in...  79.6 us

profile of v3, /device:TPU:1, one launch (start us, length us, event | category | flops | bytes accessed | tf_op | source)
XLA Modules:
  0.0 81.2 jit_solution(2606011830320482212)
XLA Ops:
  0.0 79.6 %shard_map.46 = bf16[256,256]{1,0:T(8,128)(2,1)} custom-call(bf16[256,256]{1,0:T(8,128)(2,1)} %tok_ref.1, bf16[3,512,256]{2,1,0:T(8,128)(2,1)} %bitcast.2, f32[3,7,256]{2,1,0:T(8,128)} %bitcast.3, f32[7,256]{1,0:T(8,128)} %fmix_ref.1), custom_call_target="tpu_custom_call" | custom-call | tf_op jit(solution)/shard_map/pallas_call | solution.py:247
  79.6 1.6 %copy.6 = bf16[256,256]{1,0:T(8,128)(2,1)} copy(bf16[256,256]{1,0:T(8,128)(2,1)} %shard_map.46) | data formatting | bytes 262144

commit v4 on v3

--- a/solution.py
+++ b/solution.py
@@ -15,7 +15,6 @@
 WB = 512
 CB = 256
 HALO = 16
-FAR_FIRST = (2, 1, 3)
 W_HOP = 1
 CUTS = 4
 PT = TB // CUTS
@@ -124,11 +123,42 @@
             on = send(here, here, a_send.at[way, hop, cut], a_recv.at[way, hop, cut], device)
             on.start()
             sent.append(on)
-        if hop or way == 0:
-            place = hop if way == 0 else UP + hop
-            to_side = send(here, here, s_send.at[place, cut], s_recv.at[block, cut], side)
-            to_side.start()
-            sent.append(to_side)
+
+    def to_side(way, hop):
+        here = abuf.at[lax.rem(z + NZ - hop if way == 0 else z + hop, NZ), core]
+        place = hop if way == 0 else UP + hop
+        across_chip = send(here, here, s_send.at[place], s_recv.at[lax.rem(z + NZ - hop if way == 0 else z + hop, NZ)], side)
+        across_chip.start()
+        sent.append(across_chip)
+
+    def product(strip):
+        return [jnp.dot(strip, wbuf[g], preferred_element_type=F32) for g in range(3)]
+
+    shares = []
+
+    def share_out(i, step):
+        k = lax.rem(z + step, NX)
+        distance = lax.rem(k + NX - x, NX)
+        mine, slot = distance == 0, lax.rem(distance + 3, NX)
+        for j in range(4):
+            there = abuf.at[j * 4 + k, 1 - core]
+            send(there, there, s_send.at[j * 4 + k], s_recv.at[j * 4 + k], side).wait_recv()
+        strip = jnp.concatenate([abuf[j * 4 + k, h] for j in range(4) for h in range(2)], axis=1)
+        share = send(part.at[i], landed.at[slot], p_send.at[i], p_recv.at[slot], (y * 4 + k, col))
+        sums = product(strip)
+
+        @pl.when(mine)
+        def _():
+            for g in range(3):
+                ext[HALO:, g * CB : (g + 1) * CB] = sums[g]
+
+        @pl.when(jnp.logical_not(mine))
+        def _():
+            for g in range(3):
+                part[i, :, g * CB : (g + 1) * CB] = sums[g].astype(BF16)
+            share.start()
+
+        shares.append((jnp.logical_not(mine), share))
 
     for hop in range(UP + 1):
         for cut in range(CUTS):
@@ -139,29 +169,27 @@
             pass_on(0, hop, cut)
             if hop <= DOWN:
                 pass_on(1, hop, cut)
+        to_side(0, hop)
+        if 0 < hop <= DOWN:
+            to_side(1, hop)
         if hop == W_HOP:
             w_arrival(0, 0, y_prev).wait_recv()
             on_north.start()
             w_arrival(1, 1, y_next).wait_recv()
             on_south.start()
-
-    w_stay.wait()
-    w_arrival(0, 1, y_prev).wait_recv()
-    w_arrival(1, 0, y_next).wait_recv()
-    far = lax.rem(y + 2, NY)
-    w_arrival(2, 0, far).wait_recv()
-    w_arrival(2, 1, far).wait_recv()
-    for block in range(NZ):
-        for cut in range(CUTS):
-            there = piece(block, 1 - core, cut)
-            send(there, there, s_send.at[block, cut], s_recv.at[block, cut], side).wait_recv()
-
-    def product(strip):
-        return [jnp.dot(strip, wbuf[g], preferred_element_type=F32) for g in range(3)]
-
-    def partial(k):
-        strip = jnp.concatenate([abuf[j * 4 + k, h] for j in range(4) for h in range(2)], axis=1)
-        return product(strip)
+        if hop == UP - 2:
+            w_stay.wait()
+            w_arrival(0, 1, y_prev).wait_recv()
+            w_arrival(1, 0, y_next).wait_recv()
+            far = lax.rem(y + 2, NY)
+            w_arrival(2, 0, far).wait_recv()
+            w_arrival(2, 1, far).wait_recv()
+            share_out(0, 2)
+        if hop == UP - 1:
+            share_out(1, 1)
+            share_out(2, 3)
+        if hop == UP:
+            share_out(3, 0)
 
     tails = jnp.concatenate(
         [
@@ -184,17 +212,8 @@
         rim.start()
     pl.when(first)(own_rim.start)
 
-    shares = []
-    for i, distance in enumerate(FAR_FIRST):
-        for g, block in enumerate(partial(lax.rem(x + distance, NX))):
-            part[i, :, g * CB : (g + 1) * CB] = block.astype(BF16)
-        share = send(part.at[i], landed.at[i], p_send.at[i], p_recv.at[i], across[distance - 1])
-        share.start()
-        shares.append(share)
-    for g, block in enumerate(partial(x)):
-        ext[HALO:, g * CB : (g + 1) * CB] = block
-    for i in (1, 2, 0):
-        shares[i].wait_recv()
+    for i in range(3):
+        send(landed.at[i], landed.at[i], p_send.at[i], p_recv.at[i], side).wait_recv()
     ext[HALO:, :] = ext[HALO:, :] + ((landed[1].astype(F32) + landed[2].astype(F32)) + landed[0].astype(F32))
 
     @pl.when(jnp.logical_not(first))
@@ -226,8 +245,10 @@
             mix = mix + fmix_ref[s : s + 1, at] * prod[8 - s : 8 - s + TB, at]
         out_ref[:, at] = (taps(0, lanes, HALO, TB) * mix).astype(BF16)
 
-    for share in shares + rims:
-        share.wait_send()
+    for sends, share in shares:
+        pl.when(sends)(share.wait_send)
+    for rim in rims:
+        rim.wait_send()
     pl.when(first)(own_rim.wait_send)
     for copy in w_sends + [on_north, on_south]:
         copy.wait_send()
@@ -252,14 +273,14 @@
         scratch_shapes=[
             pltpu.VMEM((NZ, 2, TB, EB), BF16),
             pltpu.VMEM((3, NY * WB, CB), BF16),
-            pltpu.VMEM((3, TB, 3 * CB), BF16),
-            pltpu.VMEM((3, TB, 3 * CB), BF16),
+            pltpu.VMEM((NX, TB, 3 * CB), BF16),
+            pltpu.VMEM((NX, TB, 3 * CB), BF16),
             pltpu.VMEM((NX, HALO, 3 * CB), BF16),
             pltpu.VMEM((NX, HALO, 3 * CB), BF16),
             pltpu.VMEM((HALO + TB, 3 * CB), F32),
             pltpu.VMEM((TB + 8, CB), F32),
-            dma, dma((CUTS,)), dma((CUTS,)), dma((2, UP, CUTS)), dma((2, UP, CUTS)), dma((NZ, CUTS)), dma((NZ, CUTS)),
-            dma, dma((3, 2)), dma((3, 2)), dma((3,)), dma((3,)), dma((NX,)), dma((NX,)),
+            dma, dma((CUTS,)), dma((CUTS,)), dma((2, UP, CUTS)), dma((2, UP, CUTS)), dma((NZ,)), dma((NZ,)),
+            dma, dma((3, 2)), dma((3, 2)), dma((NX,)), dma((NX,)), dma((NX,)), dma((NX,)),
         ],
         compiler_params=pltpu.CompilerParams(collective_id=0, has_side_effects=True),
     )(tokens, jnp.transpose(w_in, (1, 0, 2)), jnp.transpose(filt_in, (1, 0, 2)), filt_mix)

time: 81.4 us -> 80.9 us (level)
  no operation moved by 1% of the time
where the time goes in v4:
time: 80.9 us; the launch traced here: 80.8 us
  Pallas kernels  79.2 us (98%)
  local copies, waits for them, and re-layouts  1.57 us (2%)
    pallas_call x1, Pallas kernels, per_device(): pl.pallas_call(kernel, out_shape=jax.ShapeDtypeStruct((TB, CB), BF16), in...  79.2 us

profile of v4, /device:TPU:1, one launch (start us, length us, event | category | flops | bytes accessed | tf_op | source)
XLA Modules:
  0.0 80.8 jit_solution(13880500705810523204)
XLA Ops:
  0.0 79.2 %shard_map.46 = bf16[256,256]{1,0:T(8,128)(2,1)} custom-call(bf16[256,256]{1,0:T(8,128)(2,1)} %tok_ref.1, bf16[3,512,256]{2,1,0:T(8,128)(2,1)} %bitcast.2, f32[3,7,256]{2,1,0:T(8,128)} %bitcast.3, f32[7,256]{1,0:T(8,128)} %fmix_ref.1), custom_call_target="tpu_custom_call" | custom-call | tf_op jit(solution)/shard_map/pallas_call | solution.py:268
  79.2 1.6 %copy.6 = bf16[256,256]{1,0:T(8,128)(2,1)} copy(bf16[256,256]{1,0:T(8,128)(2,1)} %shard_map.46) | data formatting | bytes 262144

commit v5 on v3

--- a/solution.py
+++ b/solution.py
@@ -124,11 +124,13 @@
             on = send(here, here, a_send.at[way, hop, cut], a_recv.at[way, hop, cut], device)
             on.start()
             sent.append(on)
-        if hop or way == 0:
-            place = hop if way == 0 else UP + hop
-            to_side = send(here, here, s_send.at[place, cut], s_recv.at[block, cut], side)
-            to_side.start()
-            sent.append(to_side)
+
+    def to_side(way, hop):
+        here = abuf.at[lax.rem(z + NZ - hop if way == 0 else z + hop, NZ), core]
+        place = hop if way == 0 else UP + hop
+        across_chip = send(here, here, s_send.at[place], s_recv.at[lax.rem(z + NZ - hop if way == 0 else z + hop, NZ)], side)
+        across_chip.start()
+        sent.append(across_chip)
 
     for hop in range(UP + 1):
         for cut in range(CUTS):
@@ -139,6 +141,9 @@
             pass_on(0, hop, cut)
             if hop <= DOWN:
                 pass_on(1, hop, cut)
+        to_side(0, hop)
+        if 0 < hop <= DOWN:
+            to_side(1, hop)
         if hop == W_HOP:
             w_arrival(0, 0, y_prev).wait_recv()
             on_north.start()
@@ -152,9 +157,8 @@
     w_arrival(2, 0, far).wait_recv()
     w_arrival(2, 1, far).wait_recv()
     for block in range(NZ):
-        for cut in range(CUTS):
-            there = piece(block, 1 - core, cut)
-            send(there, there, s_send.at[block, cut], s_recv.at[block, cut], side).wait_recv()
+        there = abuf.at[block, 1 - core]
+        send(there, there, s_send.at[block], s_recv.at[block], side).wait_recv()
 
     def product(strip):
         return [jnp.dot(strip, wbuf[g], preferred_element_type=F32) for g in range(3)]
@@ -258,7 +262,7 @@
             pltpu.VMEM((NX, HALO, 3 * CB), BF16),
             pltpu.VMEM((HALO + TB, 3 * CB), F32),
             pltpu.VMEM((TB + 8, CB), F32),
-            dma, dma((CUTS,)), dma((CUTS,)), dma((2, UP, CUTS)), dma((2, UP, CUTS)), dma((NZ, CUTS)), dma((NZ, CUTS)),
+            dma, dma((CUTS,)), dma((CUTS,)), dma((2, UP, CUTS)), dma((2, UP, CUTS)), dma((NZ,)), dma((NZ,)),
             dma, dma((3, 2)), dma((3, 2)), dma((3,)), dma((3,)), dma((NX,)), dma((NX,)),
         ],
         compiler_params=pltpu.CompilerParams(collective_id=0, has_side_effects=True),

time: 81.4 us -> 80.3 us (0.986)
  Pallas kernels: 79.6 us -> 78.6 us
    pallas_call x1, Pallas kernels: 79.6 us -> 78.6 us  [per_device(): pl.pallas_call(kernel, out_shape=jax.ShapeDtypeStruct((TB, CB), BF16), in...]
where the time goes in v5:
time: 80.3 us; the launch traced here: 80.2 us
  Pallas kernels  78.6 us (98%)
  local copies, waits for them, and re-layouts  1.57 us (2%)
    pallas_call x1, Pallas kernels, per_device(): pl.pallas_call(kernel, out_shape=jax.ShapeDtypeStruct((TB, CB), BF16), in...  78.6 us

profile of v5, /device:TPU:1, one launch (start us, length us, event | category | flops | bytes accessed | tf_op | source)
XLA Modules:
  0.0 80.2 jit_solution(3225099221444333076)
XLA Ops:
  0.0 78.6 %shard_map.46 = bf16[256,256]{1,0:T(8,128)(2,1)} custom-call(bf16[256,256]{1,0:T(8,128)(2,1)} %tok_ref.1, bf16[3,512,256]{2,1,0:T(8,128)(2,1)} %bitcast.2, f32[3,7,256]{2,1,0:T(8,128)} %bitcast.3, f32[7,256]{1,0:T(8,128)} %fmix_ref.1), custom_call_target="tpu_custom_call" | custom-call | tf_op jit(solution)/shard_map/pallas_call | solution.py:251
  78.6 1.6 %copy.6 = bf16[256,256]{1,0:T(8,128)(2,1)} copy(bf16[256,256]{1,0:T(8,128)(2,1)} %shard_map.46) | data formatting | bytes 262144
